TPU v7x, 256 devices: a whole 4x4x8 slice. The times are simulated.
256 devices in a mesh: samp: 4 (over x), snp: 4 (over z_lo, core), gene: 16 (over z_hi, y).
Axes of the slice: x: 4, y: 4, z: 8 (z_hi: 4, z_lo: 2; z = z_hi * 2 + z_lo), core: 2. Of those that a mesh axis runs over, the one named last changes fastest.
Arguments:
- dosage: bfloat16 [18432, 1024], P(('samp', 'gene'), 'snp'), may hold values from 0 to 2
- snp_scale: float32 [1024], P('snp'), may hold values from 0.5 to 2
- covariates: float32 [18432, 64], P(('samp', 'gene'))
- previous: bfloat16 [18432, 1024], P(('samp', 'gene'), 'snp')
- expression: bfloat16 [18432, 20480], P('samp', 'gene')
Outputs:
- resid: bfloat16 [18432, 1024], P(('samp', 'gene'), 'snp')
- zscores: bfloat16 [1024, 20480], P('snp', 'gene')
All inputs are finite; a program needn't handle non-finite values.
Results may differ from a plain program's by a relative error of at most 0.001.
Values may be sent and summed in bfloat16 or wider, within the bound.
A program may use at most 128 MiB of HBM per device.

v0:
```python
import jax
import jax.numpy as jnp
from jax import lax
from jax.sharding import PartitionSpec as P


def cut_along(shard, dim, devices):
    shape = shard.shape
    tiles = shard.reshape(*shape[:dim], devices, shape[dim] // devices, *shape[dim + 1 :])
    return jnp.moveaxis(tiles, dim, 0)


def sum_at_owner(shard, axis, dim):
    devices = lax.axis_size(axis)
    tiles = lax.all_to_all(cut_along(shard, dim, devices), axis, 0, 0, tiled=True)
    return jnp.sum(tiles, axis=0)


def filled_up(lines, devices):
    spare = -len(lines) % devices
    return jnp.pad(lines, [(0, spare)] + [(0, 0)] * (lines.ndim - 1))


def from_everyone(shard, axis):
    copies = jnp.broadcast_to(shard, (lax.axis_size(axis), *shard.shape))
    return lax.all_to_all(copies, axis, split_axis=0, concat_axis=0, tiled=True)


def laid_out(tiles, dim):
    tiles = jnp.moveaxis(tiles, 0, dim)
    shape = tiles.shape
    return tiles.reshape(*shape[:dim], shape[dim] * shape[dim + 1], *shape[dim + 2 :])


def gather_directly(shard, axis, dim):
    tiles = from_everyone(shard, axis)
    return laid_out(tiles, dim)


def total_of(shard, axes):
    own = sum_at_owner(filled_up(shard, lax.axis_size(axes)), axes, 0)
    whole = gather_directly(own, axes, 0)
    return whole[: len(shard)].reshape(shard.shape)


def packed_total(arrays, axis):
    ends = [0]
    for a in arrays:
        ends.append(ends[-1] + a.size)
    running = total_of(jnp.concatenate([a.ravel() for a in arrays]), axis)
    return tuple((running[b:e].reshape(a.shape) for a, b, e in zip(arrays, ends, ends[1:])))


def of_everyone(shard, axis):
    everything = from_everyone(shard, axis)
    return jnp.sum(everything, axis=0)


def on_device(dosage, snp_scale, covariates, previous, expression):
    highest = lax.Precision.HIGHEST
    decoded = dosage.astype(jnp.float32) * snp_scale[None, :]
    gram = jnp.dot(covariates.T, covariates, precision=highest)
    cross = jnp.dot(covariates.T, decoded, precision=highest)
    gram, cross = packed_total((gram, cross), ("samp", "gene"))
    factor = jnp.linalg.cholesky(gram)
    coef = jax.scipy.linalg.cho_solve((factor, True), cross)
    resid = (decoded - jnp.dot(covariates, coef, precision=highest)).astype(jnp.bfloat16)
    piece = gather_directly(previous, "gene", 0)
    partial_scores = lax.dot_general(
        piece, expression, (((0,), (0,)), ((), ())), preferred_element_type=jnp.float32
    )
    x_sq = jnp.einsum("sp,sp->p", piece, piece, preferred_element_type=jnp.float32)
    scores, x_sq = (partial_scores, x_sq)
    y_sq = jnp.einsum("sg,sg->g", expression, expression, preferred_element_type=jnp.float32)
    samples = expression.shape[0] * lax.axis_size("samp")
    root = jnp.sqrt(jnp.float32(samples))
    shares, y_share = (sum_at_owner(scores, "samp", 1), sum_at_owner(y_sq, "samp", 0))
    x_sq = of_everyone(x_sq, "samp")
    denom = jnp.sqrt(x_sq + 1e-06)[:, None] * jnp.sqrt(y_share + 1e-06)[None, :]
    z_part = (root * shares / denom).astype(jnp.bfloat16)
    zscores = gather_directly(z_part, "samp", 1)
    return (resid, zscores)


def solution(mesh):
    placed = (
        P(("samp", "gene"), "snp"),
        P("snp"),
        P(("samp", "gene"), None),
        P(("samp", "gene"), "snp"),
        P("samp", "gene"),
    )
    return jax.shard_map(
        on_device,
        mesh=mesh,
        in_specs=placed,
        out_specs=(P(("samp", "gene"), "snp"), P("snp", "gene")),
        check_vma=False,
    )
```

profile of v0, /device:TPU:2, one launch (start us, length us, event | category | flops | bytes accessed | tf_op | source)
XLA Modules:
  0.0 167.5 jit_solution(1598786025547643109)
XLA Ops:
  0.7 6.8 %fusion = f32[1280]{0:T(1024)S(1)} fusion(bf16[4608,1280]{1,0:T(8,128)(2,1)} %param.9), kind=kLoop, calls=%fused_computation.1 | loop fusion | flops 17693440 | bytes 11801600 | tf_op jit(solution)/shard_map/sg,sg->g/dot_general | solution.py:74
  7.5 0.7 all_to_all.35
  8.1 5.5 %all-to-all-start.5 = ((f32[4,1,320]{2,1,0:T(1,128)}), f32[4,1,320]{2,1,0:T(1,128)S(1)}, u32[]{:S(2)}, u32[]{:S(2)}) async-start(f32[4,1,320]{2,1,0:T(1,128)} %all_to_all.35), calls=%async_computation.5 | async-start | bytes 12288 | tf_op jit(solution)/shard_map/all_to_all | solution.py:15
  13.6 0.2 fusion.12
  13.9 0.3 convolution_bitcast_fusion.2
  14.5 3.0 %all-to-all-done.5 = f32[4,1,320]{2,1,0:T(1,128)S(1)} async-done(((f32[4,1,320]{2,1,0:T(1,128)}), f32[4,1,320]{2,1,0:T(1,128)S(1)}, u32[]{:S(2)}, u32[]{:S(2)}) %all-to-all-start.5) | async-done | bytes 5152 | tf_op jit(solution)/shard_map/all_to_all | solution.py:15
  17.5 23.9 %all_to_all.45 = f32[64,1,320]{2,1,0:T(1,128)S(1)} all-to-all(f32[64,1,320]{2,1,0:T(1,128)S(1)} %all_to_all.29), channel_id=1, replica_groups=mesh['samp'=4,'snp'=4,'gene'=16] {'samp','gene'}, dimensions={0} | all-to-all | bytes 163840 | tf_op jit(solution)/shard_map/all_to_all | solution.py:15
  41.4 1.7 %broadcast_in_dim.18 = bf16[16,288,256]{2,1,0:T(8,128)(2,1)} broadcast(bf16[288,256]{1,0:T(8,128)(2,1)S(1)} %copy-done.2), dimensions={1,2} | broadcast | bytes 2506752 | tf_op jit(solution)/shard_map/broadcast_in_dim | solution.py:25
  43.1 3.7 %all-to-all-start.2 = ((bf16[16,288,256]{2,1,0:T(8,128)(2,1)}), bf16[16,288,256]{2,1,0:T(8,128)(2,1)S(1)}, u32[]{:S(2)}, u32[]{:S(2)}) async-start(bf16[16,288,256]{2,1,0:T(8,128)(2,1)} %broadcast_in_dim.18), calls=%async_computation.2 | async-start | bytes 4718592 | tf_op jit(solution)/shard_map/all_to_all | solution.py:26
  46.9 16.4 %copy.24 = bf16[4608,1280]{0,1:T(8,128)(2,1)} copy(bf16[4608,1280]{1,0:T(8,128)(2,1)} %param.9) | data formatting | bytes 23592960 | tf_op args[4]
  63.4 40.1 %all-to-all-done.2 = bf16[16,288,256]{2,1,0:T(8,128)(2,1)S(1)} async-done(((bf16[16,288,256]{2,1,0:T(8,128)(2,1)}), bf16[16,288,256]{2,1,0:T(8,128)(2,1)S(1)}, u32[]{:S(2)}, u32[]{:S(2)}) %all-to-all-start.2) | async-done | bytes 2359328 | tf_op jit(solution)/shard_map/all_to_all | solution.py:26
  103.4 0.7 broadcast_in_dim.17
  104.1 7.1 %all-to-all-start.1 = ((f32[64,1,320]{2,1,0:T(1,128)}), f32[64,1,320]{2,1,0:T(1,128)S(1)}, u32[]{:S(2)}, u32[]{:S(2)}) async-start(f32[64,1,320]{2,1,0:T(1,128)} %broadcast_in_dim.17), calls=%async_computation.1 | async-start | bytes 196608 | tf_op jit(solution)/shard_map/all_to_all | solution.py:26
  111.2 0.8 fusion.1
  112.0 10.3 %all-to-all-done.1 = f32[64,1,320]{2,1,0:T(1,128)S(1)} async-done(((f32[64,1,320]{2,1,0:T(1,128)}), f32[64,1,320]{2,1,0:T(1,128)S(1)}, u32[]{:S(2)}, u32[]{:S(2)}) %all-to-all-start.1) | async-done | bytes 81952 | tf_op jit(solution)/shard_map/all_to_all | solution.py:26
  122.3 0.6 broadcast_in_dim.19
  122.9 5.0 %all-to-all-start.4 = ((f32[4,1,256]{2,1,0:T(1,128)}), f32[4,1,256]{2,1,0:T(1,128)S(1)}, u32[]{:S(2)}, u32[]{:S(2)}) async-start(f32[4,1,256]{2,1,0:T(1,128)} %broadcast_in_dim.19), calls=%async_computation.4 | async-start | bytes 8192 | tf_op jit(solution)/shard_map/all_to_all | solution.py:26
  127.9 7.2 %convolution_bitcast_fusion = f32[4,256,320]{1,2,0:T(8,128)} fusion(bf16[4608,256,1]{1,0,2:T(8,128)(2,1)S(1)} %bitcast.49, bf16[4,320,4608]{2,1,0:T(8,128)(2,1)} %bitcast.48), kind=kOutput, calls=%fused_computation.4 | convolution fusion | flops 3019898880 | bytes 15466496 | tf_op jit(solution)/shard_map/dot_general | solution.py:69
  135.1 4.8 %all-to-all-start.3 = ((f32[4,256,320]{1,2,0:T(8,128)}), f32[4,256,320]{1,2,0:T(8,128)S(1)}, u32[]{:S(2)}, u32[]{:S(2)}) async-start(f32[4,256,320]{1,2,0:T(8,128)} %convolution_bitcast_fusion), calls=%async_computation.3 | async-start | bytes 2621440 | tf_op jit(solution)/shard_map/all_to_all | solution.py:15
  139.9 0.2 reduce.11
  140.5 5.8 %cholesky.16 = f32[64,64]{1,0:T(8,128)S(1)} custom-call(f32[64,64]{1,0:T(8,128)S(1)} %fusion.11), custom_call_target="Cholesky" | custom-call | tf_op jit(solution)/shard_map/jit(cholesky)/cholesky | solution.py:65
  146.3 0.6 compare_reduce_fusion
  147.0 0.7 fusion.7
  147.6 4.9 %custom-call.10 = f32[1,64,64]{1,2,0:T(8,128)S(1)} custom-call(f32[1,64,64]{2,1,0:T(8,128)S(1)} %fusion.7), custom_call_target="InvertDiagBlocksLowerTriangular" | custom-call | tf_op jit(solution)/shard_map/jit(_cho_solve)/triangular_solve | solution.py:66
  152.6 0.4 all-to-all-done.3
  153.2 0.9 broadcast_in_dim.20
  154.1 4.9 %all-to-all-start.6 = ((bf16[4,256,320]{1,2,0:T(8,128)(2,1)}), bf16[4,256,320]{1,2,0:T(8,128)(2,1)S(1)}, u32[]{:S(2)}, u32[]{:S(2)}) async-start(bf16[4,256,320]{1,2,0:T(8,128)(2,1)} %broadcast_in_dim.20), calls=%async_computation.6 | async-start | bytes 1310720 | tf_op jit(solution)/shard_map/all_to_all | solution.py:26
  159.0 0.3 fusion.5
  159.3 0.2 fusion.8
  159.5 1.1 fusion.3
  160.6 5.8 %all-to-all-done.6 = bf16[4,256,320]{1,2,0:T(8,128)(2,1)S(1)} async-done(((bf16[4,256,320]{1,2,0:T(8,128)(2,1)}), bf16[4,256,320]{1,2,0:T(8,128)(2,1)S(1)}, u32[]{:S(2)}, u32[]{:S(2)}) %all-to-all-start.6) | async-done | bytes 655392 | tf_op jit(solution)/shard_map/all_to_all | solution.py:26
  166.4 1.1 copy.27
  (26 shorter events, 1.0 us)
Async XLA Ops:
  0.6 13.0 %copy-start = (f32[288,64]{0,1:T(8,128)S(1)}, f32[288,64]{0,1:T(8,128)}, u32[]{:S(2)}) copy-start(f32[288,64]{0,1:T(8,128)} %param.7) | copy-start | bytes 221188
  0.6 13.2 %copy-start.1 = (bf16[288,256]{1,0:T(8,128)(2,1)S(1)}, bf16[288,256]{1,0:T(8,128)(2,1)}, u32[]{:S(2)}) copy-start(bf16[288,256]{1,0:T(8,128)(2,1)} %param.5) | copy-start | bytes 442372
  0.7 13.2 %copy-start.3 = (f32[256]{0:T(256)S(1)}, f32[256]{0:T(256)}, u32[]{:S(2)}) copy-start(f32[256]{0:T(256)} %param.6) | copy-start | bytes 3076
  0.7 40.7 %copy-start.2 = (bf16[288,256]{1,0:T(8,128)(2,1)S(1)}, bf16[288,256]{1,0:T(8,128)(2,1)}, u32[]{:S(2)}) copy-start(bf16[288,256]{1,0:T(8,128)(2,1)} %param.8) | copy-start | bytes 442372
  8.1 9.3 %all-to-all-start.5 = ((f32[4,1,320]{2,1,0:T(1,128)}), f32[4,1,320]{2,1,0:T(1,128)S(1)}, u32[]{:S(2)}, u32[]{:S(2)}) async-start(f32[4,1,320]{2,1,0:T(1,128)} %all_to_all.35), calls=%async_computation.5 | async-start | bytes 12288 | tf_op jit(solution)/shard_map/all_to_all | solution.py:15
  43.1 60.3 %all-to-all-start.2 = ((bf16[16,288,256]{2,1,0:T(8,128)(2,1)}), bf16[16,288,256]{2,1,0:T(8,128)(2,1)S(1)}, u32[]{:S(2)}, u32[]{:S(2)}) async-start(bf16[16,288,256]{2,1,0:T(8,128)(2,1)} %broadcast_in_dim.18), calls=%async_computation.2 | async-start | bytes 4718592 | tf_op jit(solution)/shard_map/all_to_all | solution.py:26
  104.1 18.2 %all-to-all-start.1 = ((f32[64,1,320]{2,1,0:T(1,128)}), f32[64,1,320]{2,1,0:T(1,128)S(1)}, u32[]{:S(2)}, u32[]{:S(2)}) async-start(f32[64,1,320]{2,1,0:T(1,128)} %broadcast_in_dim.17), calls=%async_computation.1 | async-start | bytes 196608 | tf_op jit(solution)/shard_map/all_to_all | solution.py:26
  122.9 12.2 %all-to-all-start.4 = ((f32[4,1,256]{2,1,0:T(1,128)}), f32[4,1,256]{2,1,0:T(1,128)S(1)}, u32[]{:S(2)}, u32[]{:S(2)}) async-start(f32[4,1,256]{2,1,0:T(1,128)} %broadcast_in_dim.19), calls=%async_computation.4 | async-start | bytes 8192 | tf_op jit(solution)/shard_map/all_to_all | solution.py:26
  135.1 17.9 %all-to-all-start.3 = ((f32[4,256,320]{1,2,0:T(8,128)}), f32[4,256,320]{1,2,0:T(8,128)S(1)}, u32[]{:S(2)}, u32[]{:S(2)}) async-start(f32[4,256,320]{1,2,0:T(8,128)} %convolution_bitcast_fusion), calls=%async_computation.3 | async-start | bytes 2621440 | tf_op jit(solution)/shard_map/all_to_all | solution.py:15
  154.1 12.2 %all-to-all-start.6 = ((bf16[4,256,320]{1,2,0:T(8,128)(2,1)}), bf16[4,256,320]{1,2,0:T(8,128)(2,1)S(1)}, u32[]{:S(2)}, u32[]{:S(2)}) async-start(bf16[4,256,320]{1,2,0:T(8,128)(2,1)} %broadcast_in_dim.20), calls=%async_computation.6 | async-start | bytes 1310720 | tf_op jit(solution)/shard_map/all_to_all | solution.py:26
where the time goes:
time: 168 us; the launch traced here: 167 us
  waiting for transfers between devices  59.5 us (35%)
  starting transfers between devices  31 us (18%)
  blocking collectives  23.9 us (14%)
  local copies, waits for them, and re-layouts  22.6 us (13%)
  other arithmetic  20.3 us (12%)
  matrix products  9.37 us (6%)
    all_to_all x4, waiting for transfers between devices, from_everyone(): return lax.all_to_all(copies, axis, split_axis=0, concat_axis=0, tiled=True)  56.1 us
    all_to_all x1, blocking collectives, sum_at_owner(): lax.all_to_all(cut_along(shard, dim, devices), axis, 0, 0, tiled=True)  23.9 us
    all_to_all x4, starting transfers between devices, from_everyone(): return lax.all_to_all(copies, axis, split_axis=0, concat_axis=0, tiled=True)  20.7 us
    unnamed x12, local copies, waits for them, and re-layouts  17.6 us
    all_to_all x2, starting transfers between devices, sum_at_owner(): lax.all_to_all(cut_along(shard, dim, devices), axis, 0, 0, tiled=True)  10.3 us
    dot_general x1, matrix products, on_device(): lax.dot_general(piece, expression, (((0,), (0,)), ((), ())), preferred_el...  7.21 us
    dot_general x1, other arithmetic, on_device(): jnp.einsum('sg,sg->g', expression, expression, preferred_element_type=jnp...  6.78 us
    another operation x3, other arithmetic, on_device(): factor = jnp.linalg.cholesky(gram)  6.52 us
  transfers between devices with their start and end apart: 6, of which 5 were waited for; matrix products, arithmetic and copies ran while one was open for 24% of the time, Pallas kernels for 0%

commit v1 on v0

v1 whole, which is shorter than its diff:
```python
import jax
import jax.numpy as jnp
from jax import lax
from jax.experimental import pallas as pl
from jax.experimental.pallas import tpu as pltpu
from jax.sharding import PartitionSpec as P

F32 = jnp.float32
BF16 = jnp.bfloat16
HIGHEST = lax.Precision.HIGHEST
N = 4
ROWS = 288
CUT = 144
PANEL = N * ROWS
SNP = 256
HALF = 128
GENES = 1280
WIDE = GENES + 128
SPLIT = 768
OWN = HALF // N
COVS = 64
AUG = 384
SHARE = COVS // N
SAMPLES = 18432


def kernel(
    dosage_hbm, scale_ref, cov_hbm, prev_hbm, expr_hbm,
    resid_hbm, z_hbm,
    expr, geno, dose, cov, part, from_x, from_y, from_z, sums, full, system,
    ysq, from_ysq, acc, hop1, hop2, stat, resid,
    load_sem, send, recv, store_sem,
):
    s = lax.axis_index("samp")
    gene = lax.axis_index("gene")
    zh, y = gene // N, gene % N

    def peer(axis, step):
        if axis == "x":
            return {"samp": (s + step + N) % N}
        if axis == "y":
            return {"gene": zh * N + (y + step + N) % N}
        return {"gene": ((zh + step + N) % N) * N + y}

    loads = [
        pltpu.make_async_copy(cov_hbm, cov, load_sem.at[0]),
        pltpu.make_async_copy(dosage_hbm, dose, load_sem.at[1]),
        pltpu.make_async_copy(prev_hbm.at[:, pl.ds(0, HALF)], geno.at[0, 0, pl.ds(0, ROWS)], load_sem.at[2]),
        pltpu.make_async_copy(prev_hbm.at[:, pl.ds(HALF, HALF)], geno.at[1, 0, pl.ds(0, ROWS)], load_sem.at[3]),
    ]
    for c in loads:
        c.start()
    panels = {}
    for ry in (0, 3, 1, 2):
        for rz in range(N):
            block = ((zh + rz) % N) * N + (y + ry) % N
            c = pltpu.make_async_copy(
                expr_hbm.at[pl.ds(pl.multiple_of(block * ROWS, 16), ROWS)],
                expr.at[ry, pl.ds(rz * ROWS, ROWS)],
                load_sem.at[4 + ry * N + rz],
            )
            c.start()
            panels[ry, rz] = c

    peers = [peer(a, d) for a in "xyz" for d in (1, 2, 3)]
    barrier = pltpu.get_barrier_semaphore()
    for device in peers:
        pl.semaphore_signal(barrier, inc=1, device_id=device, device_id_type=pl.DeviceIdType.MESH)

    loads[0].wait()
    loads[1].wait()
    cov_t = cov[...].T
    part[:, :SNP] = jnp.dot(cov_t, dose[...].astype(F32), precision=HIGHEST, preferred_element_type=F32)
    part[:, SNP:] = jnp.zeros((COVS, AUG - SNP), F32)
    part[:, SNP : SNP + COVS] = jnp.dot(cov_t, cov[...], precision=HIGHEST, preferred_element_type=F32)
    loads[2].wait()
    loads[3].wait()
    pl.semaphore_wait(barrier, len(peers))

    sent = []
    ids = {}

    def push(name, src, dst, axis, step):
        t = len(sent)
        c = pltpu.make_async_remote_copy(
            src_ref=src, dst_ref=dst, send_sem=send.at[t], recv_sem=recv.at[t],
            device_id=peer(axis, step), device_id_type=pl.DeviceIdType.MESH,
        )
        c.start()
        sent.append(c)
        ids[name] = c

    def arrive(*names):
        for name in names:
            ids[name].wait_recv()

    def rows(rz, lo=0, n=ROWS):
        return pl.ds(rz * ROWS + lo, n)

    def z_own(h):
        for step in (1, -1):
            to = -step % N
            push(("z", h, to), geno.at[h, 0, rows(0)], geno.at[h, 0, rows(to)], "z", step)

    def z_pass(h):
        arrive(("z", h, 3))
        push(("z", h, 2, 0), geno.at[h, 0, rows(3, 0, CUT)], geno.at[h, 0, rows(2, 0, CUT)], "z", 1)
        arrive(("z", h, 1))
        push(("z", h, 2, 1), geno.at[h, 0, rows(1, CUT, CUT)], geno.at[h, 0, rows(2, CUT, CUT)], "z", -1)

    def z_last(h):
        arrive(("z", h, 2, 0), ("z", h, 2, 1))

    def y_own(h, rz):
        for step in (1, -1):
            to = -step % N
            push(("y", h, to, rz), geno.at[h, 0, rows(rz)], geno.at[h, to, rows(rz)], "y", step)

    def y_pass(h, rz):
        arrive(("y", h, 3, rz))
        push(("y", h, 2, rz, 0), geno.at[h, 3, rows(rz, 0, CUT)], geno.at[h, 2, rows(rz, 0, CUT)], "y", 1)
        arrive(("y", h, 1, rz))
        push(("y", h, 2, rz, 1), geno.at[h, 1, rows(rz, CUT, CUT)], geno.at[h, 2, rows(rz, CUT, CUT)], "y", -1)

    def y_last(h):
        for rz in (0, 3, 1, 2):
            arrive(("y", h, 2, rz, 0), ("y", h, 2, rz, 1))

    def share(q):
        return pl.ds(pl.multiple_of(((s + q) % N) * SHARE, SHARE), SHARE)

    def cov_out():
        for q in (1, 3, 2):
            push(("cx", q), part.at[share(q)], from_x.at[q - 1], "x", q)

    def cov_step(axis_in, landed, base, slot, axis_out, landing, tag):
        arrive(*[(axis_in, q) for q in (1, 3, 2)])
        sums[slot] = base + landed[0] + landed[1] + landed[2]
        for q in (1, 3, 2):
            if landing is None:
                push((tag, q), sums.at[slot], full.at[N - q], axis_out, q)
            else:
                push((tag, q), sums.at[slot], landing.at[q - 1], axis_out, q)

    def square_block(ry, rz):
        panels[ry, rz].wait()

        def body(i, total):
            e = expr[ry, pl.ds(pl.multiple_of(rz * ROWS + i * 16, 16), 16), :].astype(F32)
            e = e * e
            return total + e[:8] + e[8:]

        ysq[...] += lax.fori_loop(0, ROWS // 16, body, jnp.zeros((8, GENES), F32), unroll=2)

    def ysq_out():
        for q in (1, 3, 2):
            push(("q", q), ysq, from_ysq.at[q - 1], "x", q)

    def scores(h, ry, first):
        lhs = geno[h, ry].T
        f = lhs.astype(F32)
        f = f * f
        squares = f[:, :128]
        for i in range(1, PANEL // 128):
            squares = squares + f[:, i * 128 : (i + 1) * 128]
        acc[h, :, GENES:] = squares if first else acc[h, :, GENES:] + squares

        @pl.loop(0, GENES // 256)
        def _(j):
            at = pl.ds(pl.multiple_of(j * 256, 256), 256)
            d = jnp.dot(lhs, expr[ry, :, at], preferred_element_type=F32)
            acc[h, :, at] = d if first else acc[h, :, at] + d

    def piece(q):
        return pl.ds(pl.multiple_of(((s + q + N) % N) * OWN, OWN), OWN)

    lo, hi = pl.ds(0, SPLIT), pl.ds(SPLIT, WIDE - SPLIT)

    def reduce_out(h):
        push(("r", h, 0), acc.at[h, piece(2), lo], hop1.at[h, :, lo], "x", 1)
        push(("r", h, 1), acc.at[h, piece(2), hi], hop1.at[h, :, hi], "x", -1)

    def reduce_pass(h):
        arrive(("r", h, 0))
        acc[h, piece(1), lo] += hop1[h, :, lo]
        push(("r2", h, 0), acc.at[h, piece(1)], hop2.at[h, 0], "x", 1)
        arrive(("r", h, 1))
        acc[h, piece(-1), hi] += hop1[h, :, hi]
        push(("r2", h, 1), acc.at[h, piece(-1)], hop2.at[h, 1], "x", -1)

    def normalise(h):
        y_total = ysq[...] + from_ysq[0] + from_ysq[1] + from_ysq[2]
        y_factor = 1.0 / jnp.sqrt(jnp.sum(y_total, axis=0, keepdims=True) + 1e-6)
        arrive(("r2", h, 0), ("r2", h, 1))
        total = acc[h, piece(0)] + hop2[h, 0] + hop2[h, 1]
        x_total = jnp.sum(total[:, GENES:], axis=1, keepdims=True)
        x_factor = jnp.sqrt(F32(SAMPLES)) / jnp.sqrt(x_total + 1e-6)
        stat[h, 0] = (total[:, :GENES] * x_factor * y_factor).astype(BF16)
        for step in (1, -1):
            push(("s", h, -step % N), stat.at[h, 0], stat.at[h, -step % N], "x", step)

    def stat_pass(h):
        half = OWN // 2
        arrive(("s", h, 3))
        push(("s", h, 2, 0), stat.at[h, 3, pl.ds(0, half)], stat.at[h, 2, pl.ds(0, half)], "x", 1)
        arrive(("s", h, 1))
        push(("s", h, 2, 1), stat.at[h, 1, pl.ds(half, half)], stat.at[h, 2, pl.ds(half, half)], "x", -1)

    stores = []

    def stat_store(h, q):
        start = pl.multiple_of(h * HALF + ((s + q) % N) * OWN, OWN)
        c = pltpu.make_async_copy(stat.at[h, q], z_hbm.at[pl.ds(start, OWN)], store_sem.at[h * N + q])
        c.start()
        stores.append(c)

    def stat_done(h):
        for q in (0, 3, 1):
            stat_store(h, q)
        arrive(("s", h, 2, 0), ("s", h, 2, 1))
        stat_store(h, 2)

    lane = lax.broadcasted_iota(jnp.int32, (COVS, 128), 1)
    line = lax.broadcasted_iota(jnp.int32, (COVS, AUG), 0)

    def gather_system():
        arrive(*[("cf", q) for q in (1, 3, 2)])
        system[share(0)] = sums[2]
        for q in (1, 2, 3):
            system[share(q)] = full[q]

    def eliminate(start, count):
        def body(k, carry):
            a = system[...]
            row = system[pl.ds(k, 1), :]
            col = jnp.sum(jnp.where(lane == k, a[:, SNP:], 0.0), axis=1, keepdims=True)
            pivot = jnp.sum(jnp.where(lane[:1] == k, row[:, SNP:], 0.0), axis=1, keepdims=True)
            row = row / pivot
            system[...] = jnp.where(line == k, row, a - col * row)
            return carry

        lax.fori_loop(start, start + count, body, 0)

    def residual():
        fit = jnp.dot(cov[...], system[:, :SNP], precision=HIGHEST, preferred_element_type=F32)
        resid[...] = ((dose[...].astype(F32) - fit) * scale_ref[...]).astype(BF16)
        c = pltpu.make_async_copy(resid, resid_hbm, store_sem.at[2 * N])
        c.start()
        stores.append(c)

    ysq[...] = jnp.zeros((8, GENES), F32)
    z_own(0)
    y_own(0, 0)
    cov_out()
    for rz in range(N):
        square_block(0, rz)
    y_pass(0, 0)
    cov_step("cx", from_x, part[share(0)], 0, "y", from_y, "cy")
    for rz in range(2):
        square_block(3, rz)
    z_pass(0)
    y_own(0, 3)
    y_own(0, 1)
    z_own(1)
    for rz in range(2, 4):
        square_block(3, rz)
    cov_step("cy", from_y, sums[0], 1, "z", from_z, "cz")
    z_last(0)
    y_own(0, 2)
    y_own(1, 0)
    y_pass(0, 3)
    for rz in range(4):
        square_block(1, rz)
    y_pass(0, 1)
    cov_step("cz", from_z, sums[1], 2, "x", None, "cf")
    z_pass(1)
    for rz in range(4):
        square_block(2, rz)
    ysq_out()
    y_own(1, 3)
    y_own(1, 1)
    y_pass(0, 2)
    scores(0, 0, True)
    z_last(1)
    y_own(1, 2)
    scores(0, 3, False)
    scores(0, 1, False)
    y_pass(1, 0)
    y_last(0)
    scores(0, 2, False)
    reduce_out(0)
    gather_system()
    eliminate(0, 16)
    y_pass(1, 3)
    eliminate(16, 8)
    reduce_pass(0)
    y_pass(1, 1)
    eliminate(24, 16)
    y_pass(1, 2)
    scores(1, 0, True)
    arrive(*[("q", q) for q in (1, 3, 2)])
    normalise(0)
    scores(1, 3, False)
    scores(1, 1, False)
    stat_pass(0)
    y_last(1)
    scores(1, 2, False)
    reduce_out(1)
    stat_done(0)
    eliminate(40, 8)
    reduce_pass(1)
    eliminate(48, 16)
    residual()
    normalise(1)
    stat_pass(1)
    stat_done(1)
    for c in sent:
        c.wait_send()
    for c in stores:
        c.wait()


N_SENDS = 71


def on_device(dosage, snp_scale, covariates, previous, expression):
    any_spec = pl.BlockSpec(memory_space=pl.ANY)
    vmem_spec = pl.BlockSpec(memory_space=pltpu.VMEM)
    return pl.pallas_call(
        kernel,
        out_shape=(
            jax.ShapeDtypeStruct((ROWS, SNP), BF16),
            jax.ShapeDtypeStruct((SNP, GENES), BF16),
        ),
        in_specs=[any_spec, vmem_spec, any_spec, any_spec, any_spec],
        out_specs=(any_spec, any_spec),
        scratch_shapes=[
            pltpu.VMEM((N, PANEL, GENES), BF16),
            pltpu.VMEM((2, N, PANEL, HALF), BF16),
            pltpu.VMEM((ROWS, SNP), BF16),
            pltpu.VMEM((ROWS, COVS), F32),
            pltpu.VMEM((COVS, AUG), F32),
            pltpu.VMEM((3, SHARE, AUG), F32),
            pltpu.VMEM((3, SHARE, AUG), F32),
            pltpu.VMEM((3, SHARE, AUG), F32),
            pltpu.VMEM((3, SHARE, AUG), F32),
            pltpu.VMEM((N, SHARE, AUG), F32),
            pltpu.VMEM((COVS, AUG), F32),
            pltpu.VMEM((8, GENES), F32),
            pltpu.VMEM((3, 8, GENES), F32),
            pltpu.VMEM((2, HALF, WIDE), F32),
            pltpu.VMEM((2, OWN, WIDE), F32),
            pltpu.VMEM((2, 2, OWN, WIDE), F32),
            pltpu.VMEM((2, N, OWN, GENES), BF16),
            pltpu.VMEM((ROWS, SNP), BF16),
            pltpu.SemaphoreType.DMA((20,)),
            pltpu.SemaphoreType.DMA((N_SENDS,)),
            pltpu.SemaphoreType.DMA((N_SENDS,)),
            pltpu.SemaphoreType.DMA((2 * N + 1,)),
        ],
        compiler_params=pltpu.CompilerParams(
            collective_id=0, has_side_effects=True, vmem_limit_bytes=48 * 1024 * 1024
        ),
    )(dosage, snp_scale[None, :], covariates, previous, expression)


def solution(mesh):
    placed = (
        P(("samp", "gene"), "snp"),
        P("snp"),
        P(("samp", "gene"), None),
        P(("samp", "gene"), "snp"),
        P("samp", "gene"),
    )
    return jax.shard_map(
        on_device,
        mesh=mesh,
        in_specs=placed,
        out_specs=(P(("samp", "gene"), "snp"), P("snp", "gene")),
        check_vma=False,
    )
```

time: 168 us -> 73 us (0.43)
  the two profiles are of different devices: /device:TPU:2 before, /device:TPU:32 now
where the time goes in v1:
time: 73 us; the launch traced here: 71.7 us
  Pallas kernels  66 us (90%)
  local copies, waits for them, and re-layouts  4.98 us (7%)
    pallas_call x1, Pallas kernels, on_device(): pl.pallas_call(kernel, out_shape=(jax.ShapeDtypeStruct((ROWS, SNP), BF16)...  66 us
    unnamed x9, local copies, waits for them, and re-layouts  4.98 us

profile of v1, /device:TPU:32, one launch (start us, length us, event | category | flops | bytes accessed | tf_op | source)
XLA Modules:
  0.0 71.7 jit_solution(14726897026970090413)
XLA Ops:
  0.6 1.0 %copy.7.cov_hbm = f32[288,64]{1,0:T(8,128)S(1)} copy(f32[288,64]{0,1:T(8,128)} %param.7) | data formatting | bytes 147456 | tf_op args[2]
  1.6 0.0 copy-start
  1.6 0.9 %copy-done = bf16[288,256]{1,0:T(8,128)(2,1)S(1)} copy-done((bf16[288,256]{1,0:T(8,128)(2,1)S(1)}, bf16[288,256]{1,0:T(8,128)(2,1)}, u32[]{:S(2)}) %copy-start) | copy-done | bytes 147480
  2.5 0.0 copy-start.1
  2.5 0.9 %copy-done.1 = bf16[288,256]{1,0:T(8,128)(2,1)S(1)} copy-done((bf16[288,256]{1,0:T(8,128)(2,1)S(1)}, bf16[288,256]{1,0:T(8,128)(2,1)}, u32[]{:S(2)}) %copy-start.1) | copy-done | bytes 147480
  3.5 0.0 copy-start.2
  3.5 0.7 copy-done.2
  4.1 66.0 %shard_map.68 = (bf16[288,256]{1,0:T(8,128)(2,1)S(1)}, bf16[256,1280]{1,0:T(8,128)(2,1)S(1)}) custom-call(bf16[288,256]{1,0:T(8,128)(2,1)S(1)} %copy-done, f32[1,256]{1,0:T(1,128)S(1)} %bitcast.1, f32[288,64]{1,0:T(8,128)S(1)} %copy.7.cov_hbm, bf16[288,256]{1,0:T(8,128)(2,1)S(1)} %copy-done.1, bf16[4608,1280]{1,0:T(8,128)(2,1)} %expr_hbm.1), custom_call_target="tpu_custom_call" | custom-call | tf_op jit(solution)/shard_map/pallas_call | solution.py:329
  70.2 0.7 copy.10
  70.8 0.8 %copy.11 = bf16[256,1280]{1,0:T(8,128)(2,1)} copy(bf16[256,1280]{1,0:T(8,128)(2,1)S(1)} %get-tuple-element.5) | data formatting | bytes 1310720
Async XLA Ops:
  1.6 0.9 %copy-start = (bf16[288,256]{1,0:T(8,128)(2,1)S(1)}, bf16[288,256]{1,0:T(8,128)(2,1)}, u32[]{:S(2)}) copy-start(bf16[288,256]{1,0:T(8,128)(2,1)} %dosage_hbm.1) | copy-start | bytes 442372
  2.5 0.9 %copy-start.1 = (bf16[288,256]{1,0:T(8,128)(2,1)S(1)}, bf16[288,256]{1,0:T(8,128)(2,1)}, u32[]{:S(2)}) copy-start(bf16[288,256]{1,0:T(8,128)(2,1)} %prev_hbm.1) | copy-start | bytes 442372
  3.5 0.7 copy-start.2

commit v2 on v1

v2 whole, which is shorter than its diff:
```python
import jax
import jax.numpy as jnp
from jax import lax
from jax.experimental import pallas as pl
from jax.experimental.pallas import tpu as pltpu
from jax.sharding import PartitionSpec as P

F32 = jnp.float32
BF16 = jnp.bfloat16
HIGHEST = lax.Precision.HIGHEST
N = 4
ROWS = 288
CUT = 144
PANEL = N * ROWS
SNP = 256
HALF = 128
GENES = 1280
TILE = 256
TILES = GENES // TILE
OWN = HALF // N
COVS = 64
AUG = 384
SHARE = COVS // N
SAMPLES = 18432


def kernel(
    dosage_hbm, scale_hbm, cov_hbm, prev_hbm, expr_hbm,
    resid_hbm, z_hbm,
    expr, geno, dose, scale, cov_t, part, from_x, from_y, from_z, sums, full, system,
    ysq, from_ysq, acc, xsq, from_acc, from_xsq, stat, resid,
    load_sem, send, recv, store_sem,
):
    s = lax.axis_index("samp")
    gene = lax.axis_index("gene")
    zh, y = gene // N, gene % N

    def peer(axis, step):
        if axis == "x":
            return {"samp": (s + step + N) % N}
        if axis == "y":
            return {"gene": zh * N + (y + step + N) % N}
        return {"gene": ((zh + step + N) % N) * N + y}

    peers = [peer(a, d) for a in "xyz" for d in (1, 2, 3)]
    barrier = pltpu.get_barrier_semaphore()
    for device in peers:
        pl.semaphore_signal(barrier, inc=1, device_id=device, device_id_type=pl.DeviceIdType.MESH)

    loads = [
        pltpu.make_async_copy(cov_hbm, cov_t, load_sem.at[0]),
        pltpu.make_async_copy(dosage_hbm, dose, load_sem.at[1]),
        pltpu.make_async_copy(prev_hbm.at[:, pl.ds(0, HALF)], geno.at[0, 0, pl.ds(0, ROWS)], load_sem.at[2]),
        pltpu.make_async_copy(prev_hbm.at[:, pl.ds(HALF, HALF)], geno.at[1, 0, pl.ds(0, ROWS)], load_sem.at[3]),
        pltpu.make_async_copy(scale_hbm, scale, load_sem.at[20]),
    ]
    for c in loads:
        c.start()
    panels = {}
    for ry in (0, 3, 1, 2):
        for rz in range(N):
            block = ((zh + rz) % N) * N + (y + ry) % N
            c = pltpu.make_async_copy(
                expr_hbm.at[pl.ds(pl.multiple_of(block * ROWS, 16), ROWS)],
                expr.at[ry, pl.ds(rz * ROWS, ROWS)],
                load_sem.at[4 + ry * N + rz],
            )
            c.start()
            panels[ry, rz] = c

    loads[0].wait()
    loads[1].wait()
    part[:, :SNP] = jnp.dot(cov_t[...], dose[...].astype(F32), precision=HIGHEST, preferred_element_type=F32)
    part[:, SNP:] = jnp.zeros((COVS, AUG - SNP), F32)
    part[:, SNP : SNP + COVS] = lax.dot_general(
        cov_t[...], cov_t[...], (((1,), (1,)), ((), ())), precision=HIGHEST, preferred_element_type=F32
    )
    ysq[...] = jnp.zeros((8, GENES), F32)
    loads[2].wait()
    loads[3].wait()
    loads[4].wait()
    pl.semaphore_wait(barrier, len(peers))

    sent = []
    ids = {}

    def push(name, src, dst, axis, step):
        t = len(sent)
        c = pltpu.make_async_remote_copy(
            src_ref=src, dst_ref=dst, send_sem=send.at[t], recv_sem=recv.at[t],
            device_id=peer(axis, step), device_id_type=pl.DeviceIdType.MESH,
        )
        c.start()
        sent.append(c)
        ids[name] = c

    def arrive(*names):
        for name in names:
            ids[name].wait_recv()

    def rows(rz, lo=0, n=ROWS):
        return pl.ds(rz * ROWS + lo, n)

    def z_send(h, *steps):
        for step in steps:
            to = -step % N
            push(("z", h, to), geno.at[h, 0, rows(0)], geno.at[h, 0, rows(to)], "z", step)

    def y_send(h, rz, *steps):
        for step in steps:
            to = -step % N
            push(("y", h, to, rz), geno.at[h, 0, rows(rz)], geno.at[h, to, rows(rz)], "y", step)

    def y_pass(h, rz):
        arrive(("y", h, 3, rz))
        push(("y", h, 2, rz, 0), geno.at[h, 3, rows(rz, 0, CUT)], geno.at[h, 2, rows(rz, 0, CUT)], "y", 1)
        arrive(("y", h, 1, rz))
        push(("y", h, 2, rz, 1), geno.at[h, 1, rows(rz, CUT, CUT)], geno.at[h, 2, rows(rz, CUT, CUT)], "y", -1)

    def y_last(h, *order):
        for rz in order:
            arrive(("y", h, 2, rz, 0), ("y", h, 2, rz, 1))

    def share(q):
        return pl.ds(pl.multiple_of(((s + q) % N) * SHARE, SHARE), SHARE)

    def cov_out():
        for q in (1, 3, 2):
            push(("cx", q), part.at[share(q)], from_x.at[q - 1], "x", q)

    def cov_step(axis_in, landed, base, slot, axis_out, landing, tag):
        arrive(*[(axis_in, q) for q in (1, 3, 2)])
        sums[slot] = base + landed[0] + landed[1] + landed[2]
        for q in (1, 3, 2):
            if landing is None:
                push((tag, q), sums.at[slot], full.at[N - q], axis_out, q)
            else:
                push((tag, q), sums.at[slot], landing.at[q - 1], axis_out, q)

    def square_block(ry, rz):
        panels[ry, rz].wait()

        def body(i, total):
            e = expr[ry, pl.ds(pl.multiple_of(rz * ROWS + i * 16, 16), 16), :].astype(F32)
            e = e * e
            return total + e[:8] + e[8:]

        ysq[...] += lax.fori_loop(0, ROWS // 16, body, jnp.zeros((8, GENES), F32), unroll=2)

    def ysq_out():
        for q in (1, 3, 2):
            push(("q", q), ysq, from_ysq.at[q - 1], "x", q)

    def piece(q):
        return pl.ds(pl.multiple_of(((s + q + N) % N) * OWN, OWN), OWN)

    def scores(h, ry, first=False, last=False):
        lhs = geno[h, ry].T
        f = lhs.astype(F32)
        f = f * f
        squares = f[:, :128]
        for i in range(1, PANEL // 128):
            squares = squares + f[:, i * 128 : (i + 1) * 128]
        xsq[h] = squares if first else xsq[h] + squares
        if last:
            for q in (2, 1, 3):
                push(("x", h, q), xsq.at[h, piece(q)], from_xsq.at[h, q - 1], "x", q)
            for j in range(TILES):
                at = pl.ds(j * TILE, TILE)
                acc[h, :, at] += jnp.dot(lhs, expr[ry, :, at], preferred_element_type=F32)
                for q in (2, 1, 3):
                    push(("r", h, j, q), acc.at[h, piece(q), at], from_acc.at[h, q - 1, :, at], "x", q)
            return

        @pl.loop(0, TILES)
        def _(j):
            at = pl.ds(pl.multiple_of(j * TILE, TILE), TILE)
            d = jnp.dot(lhs, expr[ry, :, at], preferred_element_type=F32)
            acc[h, :, at] = d if first else acc[h, :, at] + d

    stores = []

    def keep(src, dst):
        c = pltpu.make_async_copy(src, dst, store_sem.at[len(stores)])
        c.start()
        stores.append(c)

    def normalise(h):
        y_total = ysq[...] + from_ysq[0] + from_ysq[1] + from_ysq[2]
        y_factor = 1.0 / jnp.sqrt(jnp.sum(y_total, axis=0, keepdims=True) + 1e-6)
        arrive(*[("x", h, q) for q in (1, 3, 2)])
        x_total = xsq[h, piece(0)] + from_xsq[h, 0] + from_xsq[h, 1] + from_xsq[h, 2]
        x_total = jnp.sum(x_total, axis=1, keepdims=True)
        x_factor = jnp.sqrt(F32(SAMPLES)) / jnp.sqrt(x_total + 1e-6)
        out = pl.ds(pl.multiple_of(h * HALF + s * OWN, OWN), OWN)
        for j in range(TILES):
            at = pl.ds(j * TILE, TILE)
            arrive(*[("r", h, j, q) for q in (1, 3, 2)])
            total = acc[h, piece(0), at] + from_acc[h, 0, :, at] + from_acc[h, 1, :, at] + from_acc[h, 2, :, at]
            stat[h, :, at] = (total * x_factor * y_factor[:, j * TILE : (j + 1) * TILE]).astype(BF16)
            for q in (2, 1, 3):
                push(("s", h, j, q), stat.at[h, :, at], z_hbm.at[out, at], "x", q)
            keep(stat.at[h, :, at], z_hbm.at[out, at])

    def stat_done(h):
        for j in range(TILES):
            arrive(*[("s", h, j, q) for q in (1, 3, 2)])

    lane = lax.broadcasted_iota(jnp.int32, (COVS, 128), 1)
    line = lax.broadcasted_iota(jnp.int32, (COVS, AUG), 0)

    def gather_system():
        arrive(*[("cf", q) for q in (1, 3, 2)])
        system[share(0)] = sums[2]
        for q in (1, 2, 3):
            system[share(q)] = full[q]

    def eliminate(start, count):
        def body(k, carry):
            a = system[...]
            row = system[pl.ds(k, 1), :]
            col = jnp.sum(jnp.where(lane == k, a[:, SNP:], 0.0), axis=1, keepdims=True)
            pivot = jnp.sum(jnp.where(lane[:1] == k, row[:, SNP:], 0.0), axis=1, keepdims=True)
            row = row / pivot
            system[...] = jnp.where(line == k, row, a - col * row)
            return carry

        lax.fori_loop(start, start + count, body, 0)

    def residual():
        fit = lax.dot_general(
            cov_t[...], system[:, :SNP], (((0,), (0,)), ((), ())), precision=HIGHEST, preferred_element_type=F32
        )
        resid[...] = ((dose[...].astype(F32) - fit) * scale[...]).astype(BF16)
        keep(resid, resid_hbm)

    z_send(0, 1, -1)
    y_send(0, 0, 1, -1)
    cov_out()
    z_send(0, 2)
    y_send(1, 0, 1, -1)
    z_send(1, 1, -1, 2)
    for rz in range(4):
        square_block(0, rz)
    square_block(3, 0)
    y_pass(0, 0)
    cov_step("cx", from_x, part[share(0)], 0, "y", from_y, "cy")
    arrive(("z", 0, 3))
    y_send(0, 3, 1, -1)
    arrive(("z", 0, 1))
    y_send(0, 1, 1, -1)
    y_pass(1, 0)
    for rz in range(1, 4):
        square_block(3, rz)
    cov_step("cy", from_y, sums[0], 1, "z", from_z, "cz")
    for rz in range(2):
        square_block(1, rz)
    arrive(("z", 0, 2))
    y_send(0, 2, 1, -1)
    scores(0, 0, first=True)
    y_pass(0, 3)
    y_pass(0, 1)
    arrive(("z", 1, 3))
    y_send(1, 3, 1, -1)
    arrive(("z", 1, 1))
    y_send(1, 1, 1, -1)
    for rz in range(2, 4):
        square_block(1, rz)
    y_pass(0, 2)
    for rz in range(4):
        square_block(2, rz)
    ysq_out()
    arrive(("z", 1, 2))
    y_send(1, 2, 1, -1, 2)
    cov_step("cz", from_z, sums[1], 2, "x", None, "cf")
    scores(0, 3)
    scores(0, 1)
    y_last(0, 0, 3, 1, 2)
    scores(0, 2, last=True)
    y_pass(1, 3)
    y_pass(1, 1)
    scores(1, 0, first=True)
    gather_system()
    eliminate(0, 16)
    arrive(*[("y", 1, ry, 2) for ry in (3, 1)])
    scores(1, 3)
    scores(1, 1)
    arrive(*[("q", q) for q in (1, 3, 2)])
    y_last(1, 0, 3, 1)
    arrive(("y", 1, 2, 2))
    scores(1, 2, last=True)
    normalise(0)
    eliminate(16, 16)
    normalise(1)
    eliminate(32, 32)
    residual()
    stat_done(0)
    stat_done(1)
    for c in sent:
        c.wait_send()
    for c in stores:
        c.wait()


N_SENDS = 118
N_STORES = 11


def on_device(dosage, snp_scale, covariates, previous, expression):
    any_spec = pl.BlockSpec(memory_space=pl.ANY)
    return pl.pallas_call(
        kernel,
        out_shape=(
            jax.ShapeDtypeStruct((ROWS, SNP), BF16),
            jax.ShapeDtypeStruct((SNP, GENES), BF16),
        ),
        in_specs=[any_spec] * 5,
        out_specs=(any_spec, any_spec),
        scratch_shapes=[
            pltpu.VMEM((N, PANEL, GENES), BF16),
            pltpu.VMEM((2, N, PANEL, HALF), BF16),
            pltpu.VMEM((ROWS, SNP), BF16),
            pltpu.VMEM((1, SNP), F32),
            pltpu.VMEM((COVS, ROWS), F32),
            pltpu.VMEM((COVS, AUG), F32),
            pltpu.VMEM((3, SHARE, AUG), F32),
            pltpu.VMEM((3, SHARE, AUG), F32),
            pltpu.VMEM((3, SHARE, AUG), F32),
            pltpu.VMEM((3, SHARE, AUG), F32),
            pltpu.VMEM((N, SHARE, AUG), F32),
            pltpu.VMEM((COVS, AUG), F32),
            pltpu.VMEM((8, GENES), F32),
            pltpu.VMEM((3, 8, GENES), F32),
            pltpu.VMEM((2, HALF, GENES), F32),
            pltpu.VMEM((2, HALF, 128), F32),
            pltpu.VMEM((2, 3, OWN, GENES), F32),
            pltpu.VMEM((2, 3, OWN, 128), F32),
            pltpu.VMEM((2, OWN, GENES), BF16),
            pltpu.VMEM((ROWS, SNP), BF16),
            pltpu.SemaphoreType.DMA((21,)),
            pltpu.SemaphoreType.DMA((N_SENDS,)),
            pltpu.SemaphoreType.DMA((N_SENDS,)),
            pltpu.SemaphoreType.DMA((N_STORES,)),
        ],
        compiler_params=pltpu.CompilerParams(
            collective_id=0, has_side_effects=True, vmem_limit_bytes=62 * 1024 * 1024
        ),
    )(dosage, snp_scale[None, :], covariates.T, previous, expression)


def solution(mesh):
    placed = (
        P(("samp", "gene"), "snp"),
        P("snp"),
        P(("samp", "gene"), None),
        P(("samp", "gene"), "snp"),
        P("samp", "gene"),
    )
    return jax.shard_map(
        on_device,
        mesh=mesh,
        in_specs=placed,
        out_specs=(P(("samp", "gene"), "snp"), P("snp", "gene")),
        check_vma=False,
    )
```

time: 73 us -> 60.5 us (0.83); the launches traced: 71.7 us -> 60.3 us
  Pallas kernels: 66 us -> 56.2 us
  local copies, waits for them, and re-layouts: 4.98 us -> 3.55 us
    pallas_call x1, Pallas kernels: 66 us -> 56.2 us  [on_device(): pl.pallas_call(kernel, out_shape=(jax.ShapeDtypeStruct((ROWS, SNP), BF16)...]
    unnamed x9 -> x2, local copies, waits for them, and re-layouts: 4.98 us -> 3.55 us
where the time goes in v2:
time: 60.5 us; the launch traced here: 60.3 us
  Pallas kernels  56.2 us (93%)
  local copies, waits for them, and re-layouts  3.55 us (6%)
  between operations  0.64 us (1%)
    pallas_call x1, Pallas kernels, on_device(): pl.pallas_call(kernel, out_shape=(jax.ShapeDtypeStruct((ROWS, SNP), BF16)...  56.2 us
    unnamed x2, local copies, waits for them, and re-layouts  3.55 us

profile of v2, /device:TPU:32, one launch (start us, length us, event | category | flops | bytes accessed | tf_op | source)
XLA Modules:
  0.0 60.3 jit_solution(2617849116426931012)
XLA Ops:
  0.6 56.2 %shard_map.68 = (bf16[288,256]{1,0:T(8,128)(2,1)}, bf16[256,1280]{1,0:T(8,128)(2,1)}) custom-call(bf16[288,256]{1,0:T(8,128)(2,1)} %dosage_hbm.1, f32[1,256]{1,0:T(1,128)} %bitcast.3, f32[64,288]{1,0:T(8,128)} %bitcast.2, bf16[288,256]{1,0:T(8,128)(2,1)} %prev_hbm.1, bf16[4608,1280]{1,0:T(8,128)(2,1)} %expr_hbm.1), custom_call_target="tpu_custom_call" | custom-call | tf_op jit(solution)/shard_map/pallas_call | solution.py:311
  56.8 1.6 %copy.9 = bf16[288,256]{1,0:T(8,128)(2,1)} copy(bf16[288,256]{1,0:T(8,128)(2,1)} %get-tuple-element.4) | data formatting | bytes 294912
  58.4 2.0 %copy.10 = bf16[256,1280]{1,0:T(8,128)(2,1)} copy(bf16[256,1280]{1,0:T(8,128)(2,1)} %get-tuple-element.5) | data formatting | bytes 1310720

commit v3 on v2

v3 whole, which is shorter than its diff:
```python
import jax
import jax.numpy as jnp
from jax import lax
from jax.experimental import pallas as pl
from jax.experimental.pallas import tpu as pltpu
from jax.sharding import PartitionSpec as P

F32 = jnp.float32
BF16 = jnp.bfloat16
HIGHEST = lax.Precision.HIGHEST
N = 4
ROWS = 288
PACK = ROWS // 2
CUT = 80
LINES = N * PACK
PANEL = N * ROWS
SNP = 256
CHUNK = 64
CHUNKS = SNP // CHUNK
GENES = 1280
OWN = CHUNK // N
SPANS = (
    ((0, 512), (512, 768)),
    ((0, 1280),),
    ((0, 1280),),
    ((0, 256), (256, 256), (512, 256), (768, 256), (1024, 256)),
)
COVS = 64
AUG = 384
SHARE = COVS // N
SAMPLES = 18432

ORDER = (
    ("z", 0), ("y", 0, 0), ("y", 2, 0), ("z", 1), ("cov_out",), ("y", 1, 0),
    ("z", 2), ("square", 3), ("square", 0), ("cov", 0), ("y", 0, 1), ("y", 0, 2),
    ("y", 0, 3), ("square", 1), ("cov", 1), ("square", 2), ("y", 1, 1), ("z", 3),
    ("scores", 1, 0), ("ysq",), ("y", 1, 2), ("scores", 0, 0), ("y", 1, 3), ("y", 2, 3),
    ("scores", 0, 3), ("scores", 2, 0), ("scores", 0, 1), ("cov", 2), ("y", 2, 2), ("y", 2, 1),
    ("scores", 0, 2), ("scores", 1, 3), ("scores", 1, 1), ("y", 3, 0), ("y_factors",), ("y", 3, 1),
    ("y", 3, 2), ("scores", 1, 2), ("solve_in",), ("y", 3, 3), ("solve", 0), ("scores", 2, 3),
    ("scores", 2, 1), ("norm", 0), ("scores", 2, 2), ("solve", 1), ("solve", 2), ("scores", 3, 0),
    ("norm", 1), ("scores", 3, 1), ("scores", 3, 3), ("scores", 3, 2), ("solve", 3), ("solve", 4),
    ("norm", 2), ("solve", 5), ("solve", 6), ("norm", 3), ("solve", 7), ("resid",),
)
DIRECT = {(0, 0), (0, 1), (0, 2), (0, 3), (1, 0), (1, 1), (1, 2), (1, 3), (2, 0), (2, 1), (2, 2), (2, 3), (3, 0), (3, 1), (3, 2), (3, 3)}


def kernel(
    dosage_hbm, scale_hbm, cov_hbm, prev_hbm, expr_hbm,
    resid_hbm, z_hbm,
    expr, geno, prev, dose, scale, cov_t, part, from_x, from_y, from_z, sums, full, system,
    ysq, from_ysq, y_factor, acc, xsq, from_acc, stat, resid,
    load_sem, send, recv, store_sem,
):
    s = lax.axis_index("samp")
    gene = lax.axis_index("gene")
    zh, y = gene // N, gene % N

    def peer(axis, step):
        if axis == "x":
            return {"samp": (s + step + N) % N}
        if axis == "y":
            return {"gene": zh * N + (y + step + N) % N}
        return {"gene": ((zh + step + N) % N) * N + y}

    peers = [peer(a, d) for a in "xyz" for d in (1, 2, 3)]
    barrier = pltpu.get_barrier_semaphore()
    for device in peers:
        pl.semaphore_signal(barrier, inc=1, device_id=device, device_id_type=pl.DeviceIdType.MESH)

    loads = [
        pltpu.make_async_copy(prev_hbm, prev, load_sem.at[0]),
        pltpu.make_async_copy(cov_hbm, cov_t, load_sem.at[1]),
        pltpu.make_async_copy(dosage_hbm, dose, load_sem.at[2]),
        pltpu.make_async_copy(scale_hbm, scale, load_sem.at[3]),
    ]
    for c in loads:
        c.start()
    panels = {}
    for ry in (0, 3, 1, 2):
        for rz in range(N):
            block = ((zh + rz) % N) * N + (y + ry) % N
            for half in (0, 1):
                start = pl.multiple_of(block * ROWS + half * PACK, 16)
                c = pltpu.make_async_copy(
                    expr_hbm.at[pl.ds(start, PACK)],
                    expr.at[ry, pl.ds(half * LINES + rz * PACK, PACK)],
                    load_sem.at[4 + (ry * N + rz) * 2 + half],
                )
                c.start()
                panels[ry, rz, half] = c

    loads[0].wait()
    left = lax.broadcasted_iota(jnp.int32, (PACK, 2 * CHUNK), 1) < CHUNK
    spot = lax.broadcasted_iota(jnp.int32, (COVS, AUG - SNP), 1)
    squares = jnp.zeros((COVS, AUG - SNP), F32)
    for c in range(CHUNKS):
        at = pl.ds(c // 2 * 2 * CHUNK, 2 * CHUNK)
        top, bottom = prev[:PACK, at].astype(F32), prev[PACK:, at].astype(F32)
        if c % 2 == 0:
            both = jnp.where(left, top, pltpu.roll(bottom, CHUNK, 1))
        else:
            both = jnp.where(left, pltpu.roll(top, CHUNK, 1), bottom)
        geno[c, 0, :PACK] = both.astype(BF16)
        turned = both.T
        column = jnp.sum(turned * turned, axis=1, keepdims=True)
        squares = jnp.where(spot == COVS + c, column[:CHUNK] + column[CHUNK:], squares)

    loads[1].wait()
    loads[2].wait()
    part[:, :SNP] = jnp.dot(cov_t[...], dose[...].astype(F32), precision=HIGHEST, preferred_element_type=F32)
    part[:, SNP:] = squares
    part[:, SNP : SNP + COVS] = lax.dot_general(
        cov_t[...], cov_t[...], (((1,), (1,)), ((), ())), precision=HIGHEST, preferred_element_type=F32
    )
    ysq[...] = jnp.zeros((1, GENES), F32)
    loads[3].wait()
    pl.semaphore_wait(barrier, len(peers))

    sent = []
    ids = {}

    def push(name, src, dst, axis, step):
        t = len(sent)
        c = pltpu.make_async_remote_copy(
            src_ref=src, dst_ref=dst, send_sem=send.at[t], recv_sem=recv.at[t],
            device_id=peer(axis, step), device_id_type=pl.DeviceIdType.MESH,
        )
        c.start()
        sent.append(c)
        ids[name] = c

    landed = set()

    def arrive(*names):
        for name in names:
            if name not in landed:
                ids[name].wait_recv()
                landed.add(name)

    def rows(rz, lo=0, n=PACK):
        return pl.ds(rz * PACK + lo, n)

    def z_send(c):
        for step in (1, -1, 2):
            to = -step % N
            push(("z", c, to), geno.at[c, 0, rows(0)], geno.at[c, 0, rows(to)], "z", step)

    def y_go(c, rz):
        if rz:
            arrive(("z", c, rz))
        for step in (1, -1, 2) if (c, rz) in DIRECT else (1, -1):
            to = -step % N
            push(("y", c, to, rz), geno.at[c, 0, rows(rz)], geno.at[c, to, rows(rz)], "y", step)

    def y_pass(c, rz):
        arrive(("y", c, 3, rz))
        push(("y", c, 2, rz, 0), geno.at[c, 3, rows(rz, 0, CUT)], geno.at[c, 2, rows(rz, 0, CUT)], "y", 1)
        arrive(("y", c, 1, rz))
        push(("y", c, 2, rz, 1), geno.at[c, 1, rows(rz, CUT, PACK - CUT)], geno.at[c, 2, rows(rz, CUT, PACK - CUT)], "y", -1)

    def panel_arrive(c, ry):
        for rz in (0, 3, 1, 2):
            if ry == 0 and rz:
                arrive(("z", c, rz))
            elif ry in (1, 3) or (ry and (c, rz) in DIRECT):
                arrive(("y", c, ry, rz))
            elif ry:
                arrive(("y", c, 2, rz, 0), ("y", c, 2, rz, 1))

    def share(q):
        return pl.ds(pl.multiple_of(((s + q) % N) * SHARE, SHARE), SHARE)

    def cov_out():
        for q in (1, 3, 2):
            push(("cx", q), part.at[share(q)], from_x.at[q - 1], "x", q)

    def cov(i):
        tag, landing, base = (("cx", from_x, part.at[share(0)]), ("cy", from_y, sums.at[0]), ("cz", from_z, sums.at[1]))[i]
        arrive(*[(tag, q) for q in (1, 3, 2)])
        sums[i] = base[...] + landing[0] + landing[1] + landing[2]
        for q in (1, 3, 2):
            if i == 0:
                push(("cy", q), sums.at[0], from_y.at[q - 1], "y", q)
            elif i == 1:
                push(("cz", q), sums.at[1], from_z.at[q - 1], "z", q)
            else:
                push(("cf", q), sums.at[2], full.at[N - q], "x", q)

    seen = set()

    def square(ry):
        total = jnp.zeros((8, GENES), F32)
        for half in (0, 1):
            for rz in range(N):
                if (ry, rz) not in seen:
                    panels[ry, rz, half].wait()

            def body(i, total):
                e = expr[ry, pl.ds(pl.multiple_of(half * LINES + i * 16, 16), 16), :].astype(F32)
                e = e * e
                return total + e[:8] + e[8:]

            total = lax.fori_loop(0, LINES // 16, body, total, unroll=3)
        seen.update((ry, rz) for rz in range(N))
        ysq[...] += jnp.sum(total, axis=0, keepdims=True)

    def ysq_out():
        for q in (1, 3, 2):
            push(("q", q), ysq, from_ysq.at[q - 1], "x", q)

    def piece(q):
        return pl.ds(pl.multiple_of(((s + q) % N) * OWN, OWN), OWN)

    begun = set()

    def scores(c, ry):
        first, last = c not in begun, ry == 2
        begun.add(c)
        for rz in range(N):
            for half in (0, 1):
                if (ry, rz) not in seen:
                    panels[ry, rz, half].wait()
            seen.add((ry, rz))
        panel_arrive(c, ry)
        packed = geno[c, ry].astype(F32)
        lhs = jnp.concatenate([packed, pltpu.roll(packed, CHUNK, 1)], axis=0).astype(BF16).T[:CHUNK]
        for j, (start, size) in enumerate(SPANS[c] if last else SPANS[3]):
            at = pl.ds(start, size)
            d = jnp.dot(lhs, expr[ry, :, at], preferred_element_type=F32)
            acc[c, :, at] = d if first else acc[c, :, at] + d
            if last:
                for q in (2, 1, 3):
                    push(("r", c, j, q), acc.at[c, piece(q), at], from_acc.at[c, q - 1, :, at], "x", q)

    stores = []

    def keep(src, dst):
        c = pltpu.make_async_copy(src, dst, store_sem.at[len(stores)])
        c.start()
        stores.append(c)

    def normalise(c):
        x_total = xsq[piece(0), :][:, COVS + c : COVS + c + 1]
        x_factor = jnp.sqrt(F32(SAMPLES)) / jnp.sqrt(x_total + 1e-6)
        out = pl.ds(pl.multiple_of(c * CHUNK + s * OWN, OWN), OWN)
        for j, (start, size) in enumerate(SPANS[c]):
            at = pl.ds(start, size)
            arrive(*[("r", c, j, q) for q in (1, 3, 2)])
            total = acc[c, piece(0), at] + from_acc[c, 0, :, at] + from_acc[c, 1, :, at] + from_acc[c, 2, :, at]
            stat[c, :, at] = (total * x_factor * y_factor[:, at]).astype(BF16)
            for q in (2, 1, 3):
                push(("s", c, j, q), stat.at[c, :, at], z_hbm.at[out, at], "x", q)
            keep(stat.at[c, :, at], z_hbm.at[out, at])

    def y_factors():
        arrive(*[("q", q) for q in (1, 3, 2)])
        y_total = ysq[...] + from_ysq[0] + from_ysq[1] + from_ysq[2]
        y_factor[...] = 1.0 / jnp.sqrt(y_total + 1e-6)

    def stat_done(c):
        for j in range(len(SPANS[c])):
            arrive(*[("s", c, j, q) for q in (1, 3, 2)])

    lane = lax.broadcasted_iota(jnp.int32, (COVS, 128), 1)
    line = lax.broadcasted_iota(jnp.int32, (COVS, AUG), 0)

    def solve_in():
        arrive(*[("cf", q) for q in (1, 3, 2)])
        system[share(0)] = sums[2]
        for q in (1, 2, 3):
            system[share(q)] = full[q]
        xsq[...] = system[:, SNP:]

    def eliminate(i):
        start, count = i * 8, 8

        def body(k, carry):
            a = system[...]
            row = system[pl.ds(k, 1), :]
            col = jnp.sum(jnp.where(lane == k, a[:, SNP:], 0.0), axis=1, keepdims=True)
            pivot = jnp.sum(jnp.where(lane[:1] == k, row[:, SNP:], 0.0), axis=1, keepdims=True)
            row = row / pivot
            system[...] = jnp.where(line == k, row, a - col * row)
            return carry

        lax.fori_loop(start, start + count, body, 0)

    def residual():
        fit = lax.dot_general(
            cov_t[...], system[:, :SNP], (((0,), (0,)), ((), ())), precision=HIGHEST, preferred_element_type=F32
        )
        resid[...] = ((dose[...].astype(F32) - fit) * scale[...]).astype(BF16)
        keep(resid, resid_hbm)

    steps = {
        "z": z_send, "y": y_go, "pass": y_pass, "cov_out": cov_out, "cov": cov, "square": square, "ysq": ysq_out,
        "y_factors": y_factors, "solve_in": solve_in, "solve": eliminate, "resid": residual, "scores": scores, "norm": normalise,
    }
    for name, *at in ORDER:
        steps[name](*at)
    for c in range(CHUNKS):
        stat_done(c)
    for c in sent:
        c.wait_send()
    for c in stores:
        c.wait()


N_SENDS = 129
N_STORES = 10


def on_device(dosage, snp_scale, covariates, previous, expression):
    any_spec = pl.BlockSpec(memory_space=pl.ANY)
    return pl.pallas_call(
        kernel,
        out_shape=(
            jax.ShapeDtypeStruct((ROWS, SNP), BF16),
            jax.ShapeDtypeStruct((SNP, GENES), BF16),
        ),
        in_specs=[any_spec] * 5,
        out_specs=(any_spec, any_spec),
        scratch_shapes=[
            pltpu.VMEM((N, PANEL, GENES), BF16),
            pltpu.VMEM((CHUNKS, N, LINES, 2 * CHUNK), BF16),
            pltpu.VMEM((ROWS, SNP), BF16),
            pltpu.VMEM((ROWS, SNP), BF16),
            pltpu.VMEM((1, SNP), F32),
            pltpu.VMEM((COVS, ROWS), F32),
            pltpu.VMEM((COVS, AUG), F32),
            pltpu.VMEM((3, SHARE, AUG), F32),
            pltpu.VMEM((3, SHARE, AUG), F32),
            pltpu.VMEM((3, SHARE, AUG), F32),
            pltpu.VMEM((3, SHARE, AUG), F32),
            pltpu.VMEM((N, SHARE, AUG), F32),
            pltpu.VMEM((COVS, AUG), F32),
            pltpu.VMEM((1, GENES), F32),
            pltpu.VMEM((3, 1, GENES), F32),
            pltpu.VMEM((1, GENES), F32),
            pltpu.VMEM((CHUNKS, CHUNK, GENES), F32),
            pltpu.VMEM((COVS, AUG - SNP), F32),
            pltpu.VMEM((CHUNKS, 3, OWN, GENES), F32),
            pltpu.VMEM((CHUNKS, OWN, GENES), BF16),
            pltpu.VMEM((ROWS, SNP), BF16),
            pltpu.SemaphoreType.DMA((36,)),
            pltpu.SemaphoreType.DMA((N_SENDS,)),
            pltpu.SemaphoreType.DMA((N_SENDS,)),
            pltpu.SemaphoreType.DMA((N_STORES,)),
        ],
        compiler_params=pltpu.CompilerParams(
            collective_id=0, has_side_effects=True, vmem_limit_bytes=62 * 1024 * 1024
        ),
    )(dosage, snp_scale[None, :], covariates.T, previous, expression)


def solution(mesh):
    placed = (
        P(("samp", "gene"), "snp"),
        P("snp"),
        P(("samp", "gene"), None),
        P(("samp", "gene"), "snp"),
        P("samp", "gene"),
    )
    return jax.shard_map(
        on_device,
        mesh=mesh,
        in_specs=placed,
        out_specs=(P(("samp", "gene"), "snp"), P("snp", "gene")),
        check_vma=False,
    )
```

time: 60.5 us -> 57.9 us (0.957)
  Pallas kernels: 56.2 us -> 53.5 us
    pallas_call x1, Pallas kernels: 56.2 us -> 53.5 us  [on_device(): pl.pallas_call(kernel, out_shape=(jax.ShapeDtypeStruct((ROWS, SNP), BF16)...]
where the time goes in v3:
time: 57.9 us; the launch traced here: 57.7 us
  Pallas kernels  53.5 us (92%)
  local copies, waits for them, and re-layouts  3.55 us (6%)
  between operations  0.64 us (1%)
    pallas_call x1, Pallas kernels, on_device(): pl.pallas_call(kernel, out_shape=(jax.ShapeDtypeStruct((ROWS, SNP), BF16)...  53.5 us
    unnamed x2, local copies, waits for them, and re-layouts  3.55 us

profile of v3, /device:TPU:32, one launch (start us, length us, event | category | flops | bytes accessed | tf_op | source)
XLA Modules:
  0.0 57.7 jit_solution(11849886808136149843)
XLA Ops:
  0.6 53.5 %shard_map.68 = (bf16[288,256]{1,0:T(8,128)(2,1)}, bf16[256,1280]{1,0:T(8,128)(2,1)}) custom-call(bf16[288,256]{1,0:T(8,128)(2,1)} %dosage_hbm.1, f32[1,256]{1,0:T(1,128)} %bitcast.3, f32[64,288]{1,0:T(8,128)} %bitcast.2, bf16[288,256]{1,0:T(8,128)(2,1)} %prev_hbm.1, bf16[4608,1280]{1,0:T(8,128)(2,1)} %expr_hbm.1), custom_call_target="tpu_custom_call" | custom-call | tf_op jit(solution)/shard_map/pallas_call | solution.py:316
  54.2 1.6 %copy.9 = bf16[288,256]{1,0:T(8,128)(2,1)} copy(bf16[288,256]{1,0:T(8,128)(2,1)} %get-tuple-element.4) | data formatting | bytes 294912
  55.7 2.0 %copy.10 = bf16[256,1280]{1,0:T(8,128)(2,1)} copy(bf16[256,1280]{1,0:T(8,128)(2,1)} %get-tuple-element.5) | data formatting | bytes 1310720

commit v4 on v3

--- a/solution.py
+++ b/solution.py
@@ -31,16 +31,16 @@
 SAMPLES = 18432
 
 ORDER = (
-    ("z", 0), ("y", 0, 0), ("y", 2, 0), ("z", 1), ("cov_out",), ("y", 1, 0),
-    ("z", 2), ("square", 3), ("square", 0), ("cov", 0), ("y", 0, 1), ("y", 0, 2),
-    ("y", 0, 3), ("square", 1), ("cov", 1), ("square", 2), ("y", 1, 1), ("z", 3),
-    ("scores", 1, 0), ("ysq",), ("y", 1, 2), ("scores", 0, 0), ("y", 1, 3), ("y", 2, 3),
-    ("scores", 0, 3), ("scores", 2, 0), ("scores", 0, 1), ("cov", 2), ("y", 2, 2), ("y", 2, 1),
-    ("scores", 0, 2), ("scores", 1, 3), ("scores", 1, 1), ("y", 3, 0), ("y_factors",), ("y", 3, 1),
-    ("y", 3, 2), ("scores", 1, 2), ("solve_in",), ("y", 3, 3), ("solve", 0), ("scores", 2, 3),
-    ("scores", 2, 1), ("norm", 0), ("scores", 2, 2), ("solve", 1), ("solve", 2), ("scores", 3, 0),
-    ("norm", 1), ("scores", 3, 1), ("scores", 3, 3), ("scores", 3, 2), ("solve", 3), ("solve", 4),
-    ("norm", 2), ("solve", 5), ("solve", 6), ("norm", 3), ("solve", 7), ("resid",),
+    ("z", 0), ("y", 0, 0), ("y", 1, 0), ("y", 2, 0), ("cov_out",), ("square", 0),
+    ("square", 3), ("square", 2), ("z", 1), ("cov", 0), ("y", 0, 3), ("z", 2),
+    ("y", 0, 1), ("cov", 1), ("y", 0, 2), ("square", 1), ("scores", 0, 0), ("y", 1, 2),
+    ("y", 1, 3), ("y", 1, 1), ("scores", 1, 0), ("ysq",), ("z", 3), ("scores", 0, 1),
+    ("scores", 0, 3), ("y", 2, 1), ("cov", 2), ("y", 2, 2), ("y", 2, 3), ("y_factors",),
+    ("scores", 0, 2), ("scores", 2, 0), ("scores", 1, 1), ("scores", 1, 3), ("y", 3, 3), ("y", 3, 0),
+    ("solve_in",), ("y", 3, 1), ("y", 3, 2), ("scores", 1, 2), ("solve", 0), ("scores", 3, 0),
+    ("scores", 2, 3), ("norm", 0), ("scores", 2, 1), ("scores", 2, 2), ("solve", 1), ("solve", 2),
+    ("norm", 1), ("scores", 3, 3), ("scores", 3, 1), ("scores", 3, 2), ("solve", 3), ("solve", 4),
+    ("solve", 5), ("norm", 2), ("solve", 6), ("norm", 3), ("solve", 7), ("resid",),
 )
 DIRECT = {(0, 0), (0, 1), (0, 2), (0, 3), (1, 0), (1, 1), (1, 2), (1, 3), (2, 0), (2, 1), (2, 2), (2, 3), (3, 0), (3, 1), (3, 2), (3, 3)}
 
@@ -201,7 +201,7 @@
                 e = e * e
                 return total + e[:8] + e[8:]
 
-            total = lax.fori_loop(0, LINES // 16, body, total, unroll=3)
+            total = lax.fori_loop(0, LINES // 16, body, total, unroll=6)
         seen.update((ry, rz) for rz in range(N))
         ysq[...] += jnp.sum(total, axis=0, keepdims=True)
 
@@ -223,8 +223,8 @@
                     panels[ry, rz, half].wait()
             seen.add((ry, rz))
         panel_arrive(c, ry)
-        packed = geno[c, ry].astype(F32)
-        lhs = jnp.concatenate([packed, pltpu.roll(packed, CHUNK, 1)], axis=0).astype(BF16).T[:CHUNK]
+        turned = geno[c, ry].T
+        lhs = jnp.concatenate([turned[:CHUNK], turned[CHUNK:]], axis=1)
         for j, (start, size) in enumerate(SPANS[c] if last else SPANS[3]):
             at = pl.ds(start, size)
             d = jnp.dot(lhs, expr[ry, :, at], preferred_element_type=F32)
@@ -311,9 +311,25 @@
 N_STORES = 10
 
 
+def keep_all(resid_in, z_in, resid_out, z_out, resid_held, z_held, in_sem, out_sem):
+    ways = [(resid_in, resid_held, resid_out)]
+    for i in range(N):
+        at = pl.ds(i * CHUNK, CHUNK)
+        ways.append((z_in.at[at], z_held.at[at], z_out.at[at]))
+    ins = [pltpu.make_async_copy(a, b, in_sem.at[i]) for i, (a, b, _) in enumerate(ways)]
+    outs = [pltpu.make_async_copy(b, c, out_sem.at[i]) for i, (_, b, c) in enumerate(ways)]
+    for copy in ins:
+        copy.start()
+    for first, then in zip(ins, outs):
+        first.wait()
+        then.start()
+    for copy in outs:
+        copy.wait()
+
+
 def on_device(dosage, snp_scale, covariates, previous, expression):
     any_spec = pl.BlockSpec(memory_space=pl.ANY)
-    return pl.pallas_call(
+    resid, z = pl.pallas_call(
         kernel,
         out_shape=(
             jax.ShapeDtypeStruct((ROWS, SNP), BF16),
@@ -352,6 +368,22 @@
             collective_id=0, has_side_effects=True, vmem_limit_bytes=62 * 1024 * 1024
         ),
     )(dosage, snp_scale[None, :], covariates.T, previous, expression)
+    return pl.pallas_call(
+        keep_all,
+        out_shape=(
+            jax.ShapeDtypeStruct((ROWS, SNP), BF16),
+            jax.ShapeDtypeStruct((SNP, GENES), BF16),
+        ),
+        in_specs=[any_spec] * 2,
+        out_specs=(any_spec, any_spec),
+        scratch_shapes=[
+            pltpu.VMEM((ROWS, SNP), BF16),
+            pltpu.VMEM((SNP, GENES), BF16),
+            pltpu.SemaphoreType.DMA((N + 1,)),
+            pltpu.SemaphoreType.DMA((N + 1,)),
+        ],
+        compiler_params=pltpu.CompilerParams(vmem_limit_bytes=62 * 1024 * 1024),
+    )(resid, z)
 
 
 def solution(mesh):

time: 57.9 us -> 54.7 us (0.945); the launches traced: 57.7 us -> 53.6 us
  local copies, waits for them, and re-layouts: 3.55 us -> 0 us
    unnamed x2 -> x0, local copies, waits for them, and re-layouts: 3.55 us -> none
    pallas_call x1, Pallas kernels: 53.5 us -> 51 us  [on_device(): pl.pallas_call(kernel, out_shape=(jax.ShapeDtypeStruct((ROWS, SNP), BF16)...]
    pallas_call x0 -> x1, Pallas kernels: none -> 1.98 us  [on_device(): pl.pallas_call(keep_all, out_shape=(jax.ShapeDtypeStruct((ROWS, SNP), BF1...]
where the time goes in v4:
time: 54.7 us; the launch traced here: 53.6 us
  Pallas kernels  53 us (97%)
  between operations  0.64 us (1%)
    pallas_call x1, Pallas kernels, on_device(): pl.pallas_call(kernel, out_shape=(jax.ShapeDtypeStruct((ROWS, SNP), BF16)...  51 us
    pallas_call x1, Pallas kernels, on_device(): pl.pallas_call(keep_all, out_shape=(jax.ShapeDtypeStruct((ROWS, SNP), BF1...  1.98 us

profile of v4, /device:TPU:32, one launch (start us, length us, event | category | flops | bytes accessed | tf_op | source)
XLA Modules:
  0.0 53.6 jit_solution(15588256325214927763)
XLA Ops:
  0.6 51.0 %shard_map.68 = (bf16[288,256]{1,0:T(8,128)(2,1)}, bf16[256,1280]{1,0:T(8,128)(2,1)}) custom-call(bf16[288,256]{1,0:T(8,128)(2,1)} %dosage_hbm.1, f32[1,256]{1,0:T(1,128)} %bitcast.3, f32[64,288]{1,0:T(8,128)} %bitcast.2, bf16[288,256]{1,0:T(8,128)(2,1)} %prev_hbm.1, bf16[4608,1280]{1,0:T(8,128)(2,1)} %expr_hbm.1), custom_call_target="tpu_custom_call" | custom-call | tf_op jit(solution)/shard_map/pallas_call | solution.py:332
  51.6 2.0 %shard_map.69 = (bf16[288,256]{1,0:T(8,128)(2,1)}, bf16[256,1280]{1,0:T(8,128)(2,1)}) custom-call(bf16[288,256]{1,0:T(8,128)(2,1)} %get-tuple-element.4.resid_in, bf16[256,1280]{1,0:T(8,128)(2,1)} %get-tuple-element.5.z_in), custom_call_target="tpu_custom_call" | custom-call | tf_op jit(solution)/shard_map/pallas_call | solution.py:371

commit v5 on v4

--- a/solution.py
+++ b/solution.py
@@ -31,16 +31,16 @@
 SAMPLES = 18432
 
 ORDER = (
-    ("z", 0), ("y", 0, 0), ("y", 1, 0), ("y", 2, 0), ("cov_out",), ("square", 0),
-    ("square", 3), ("square", 2), ("z", 1), ("cov", 0), ("y", 0, 3), ("z", 2),
-    ("y", 0, 1), ("cov", 1), ("y", 0, 2), ("square", 1), ("scores", 0, 0), ("y", 1, 2),
-    ("y", 1, 3), ("y", 1, 1), ("scores", 1, 0), ("ysq",), ("z", 3), ("scores", 0, 1),
-    ("scores", 0, 3), ("y", 2, 1), ("cov", 2), ("y", 2, 2), ("y", 2, 3), ("y_factors",),
-    ("scores", 0, 2), ("scores", 2, 0), ("scores", 1, 1), ("scores", 1, 3), ("y", 3, 3), ("y", 3, 0),
-    ("solve_in",), ("y", 3, 1), ("y", 3, 2), ("scores", 1, 2), ("solve", 0), ("scores", 3, 0),
-    ("scores", 2, 3), ("norm", 0), ("scores", 2, 1), ("scores", 2, 2), ("solve", 1), ("solve", 2),
-    ("norm", 1), ("scores", 3, 3), ("scores", 3, 1), ("scores", 3, 2), ("solve", 3), ("solve", 4),
-    ("solve", 5), ("norm", 2), ("solve", 6), ("norm", 3), ("solve", 7), ("resid",),
+    ("z", 1), ("y", 2, 0), ("cov_out",), ("y", 1, 0), ("square", 3), ("square", 2),
+    ("y", 0, 0), ("z", 2), ("cov", 0), ("square", 1), ("y", 1, 1), ("y", 1, 3),
+    ("y", 1, 2), ("z", 0), ("square", 0), ("cov", 1), ("y", 2, 2), ("ysq",),
+    ("scores", 2, 0), ("y", 2, 1), ("scores", 1, 0), ("y", 2, 3), ("z", 3), ("y_factors",),
+    ("scores", 1, 3), ("scores", 1, 1), ("y", 0, 1), ("cov", 2), ("y", 0, 3), ("scores", 1, 2),
+    ("scores", 0, 0), ("y", 0, 2), ("scores", 2, 1), ("scores", 2, 3), ("y", 3, 1), ("scores", 2, 2),
+    ("scores", 3, 0), ("y", 3, 3), ("y", 3, 0), ("solve_in",), ("y", 3, 2), ("solve", 0),
+    ("scores", 0, 1), ("norm", 1), ("scores", 0, 3), ("scores", 0, 2), ("solve", 1), ("norm", 2),
+    ("solve", 2), ("scores", 3, 3), ("scores", 3, 1), ("scores", 3, 2), ("flush", 30), ("solve", 3), ("solve", 4),
+    ("solve", 5), ("norm", 0), ("solve", 6), ("norm", 3), ("solve", 7), ("resid",),
 )
 DIRECT = {(0, 0), (0, 1), (0, 2), (0, 3), (1, 0), (1, 1), (1, 2), (1, 3), (2, 0), (2, 1), (2, 2), (2, 3), (3, 0), (3, 1), (3, 2), (3, 3)}
 
@@ -92,8 +92,6 @@
 
     loads[0].wait()
     left = lax.broadcasted_iota(jnp.int32, (PACK, 2 * CHUNK), 1) < CHUNK
-    spot = lax.broadcasted_iota(jnp.int32, (COVS, AUG - SNP), 1)
-    squares = jnp.zeros((COVS, AUG - SNP), F32)
     for c in range(CHUNKS):
         at = pl.ds(c // 2 * 2 * CHUNK, 2 * CHUNK)
         top, bottom = prev[:PACK, at].astype(F32), prev[PACK:, at].astype(F32)
@@ -102,19 +100,7 @@
         else:
             both = jnp.where(left, pltpu.roll(top, CHUNK, 1), bottom)
         geno[c, 0, :PACK] = both.astype(BF16)
-        turned = both.T
-        column = jnp.sum(turned * turned, axis=1, keepdims=True)
-        squares = jnp.where(spot == COVS + c, column[:CHUNK] + column[CHUNK:], squares)
-
-    loads[1].wait()
-    loads[2].wait()
-    part[:, :SNP] = jnp.dot(cov_t[...], dose[...].astype(F32), precision=HIGHEST, preferred_element_type=F32)
-    part[:, SNP:] = squares
-    part[:, SNP : SNP + COVS] = lax.dot_general(
-        cov_t[...], cov_t[...], (((1,), (1,)), ((), ())), precision=HIGHEST, preferred_element_type=F32
-    )
     ysq[...] = jnp.zeros((1, GENES), F32)
-    loads[3].wait()
     pl.semaphore_wait(barrier, len(peers))
 
     sent = []
@@ -172,6 +158,19 @@
         return pl.ds(pl.multiple_of(((s + q) % N) * SHARE, SHARE), SHARE)
 
     def cov_out():
+        spot = lax.broadcasted_iota(jnp.int32, (COVS, AUG - SNP), 1)
+        squares = jnp.zeros((COVS, AUG - SNP), F32)
+        for c in range(CHUNKS):
+            turned = geno[c, 0, :PACK].astype(F32).T
+            column = jnp.sum(turned * turned, axis=1, keepdims=True)
+            squares = jnp.where(spot == COVS + c, column[:CHUNK] + column[CHUNK:], squares)
+        for c in loads[1:]:
+            c.wait()
+        part[:, :SNP] = jnp.dot(cov_t[...], dose[...].astype(F32), precision=HIGHEST, preferred_element_type=F32)
+        part[:, SNP:] = squares
+        part[:, SNP : SNP + COVS] = lax.dot_general(
+            cov_t[...], cov_t[...], (((1,), (1,)), ((), ())), precision=HIGHEST, preferred_element_type=F32
+        )
         for q in (1, 3, 2):
             push(("cx", q), part.at[share(q)], from_x.at[q - 1], "x", q)
 
@@ -262,6 +261,13 @@
         for j in range(len(SPANS[c])):
             arrive(*[("s", c, j, q) for q in (1, 3, 2)])
 
+    flushed = []
+
+    def flush(recent=0):
+        for c in sent[len(flushed) : len(sent) - recent]:
+            c.wait_send()
+            flushed.append(c)
+
     lane = lax.broadcasted_iota(jnp.int32, (COVS, 128), 1)
     line = lax.broadcasted_iota(jnp.int32, (COVS, AUG), 0)
 
@@ -295,14 +301,13 @@
 
     steps = {
         "z": z_send, "y": y_go, "pass": y_pass, "cov_out": cov_out, "cov": cov, "square": square, "ysq": ysq_out,
-        "y_factors": y_factors, "solve_in": solve_in, "solve": eliminate, "resid": residual, "scores": scores, "norm": normalise,
+        "y_factors": y_factors, "solve_in": solve_in, "solve": eliminate, "resid": residual, "scores": scores, "norm": normalise, "flush": flush,
     }
     for name, *at in ORDER:
         steps[name](*at)
     for c in range(CHUNKS):
         stat_done(c)
-    for c in sent:
-        c.wait_send()
+    flush()
     for c in stores:
         c.wait()
 

time: 54.7 us -> 54.5 us (level)
  no operation moved by 1% of the time
where the time goes in v5:
time: 54.5 us; the launch traced here: 53.8 us
  Pallas kernels  53.2 us (98%)
  between operations  0.64 us (1%)
    pallas_call x1, Pallas kernels, on_device(): pl.pallas_call(kernel, out_shape=(jax.ShapeDtypeStruct((ROWS, SNP), BF16)...  51.2 us
    pallas_call x1, Pallas kernels, on_device(): pl.pallas_call(keep_all, out_shape=(jax.ShapeDtypeStruct((ROWS, SNP), BF1...  1.98 us

profile of v5, /device:TPU:32, one launch (start us, length us, event | category | flops | bytes accessed | tf_op | source)
XLA Modules:
  0.0 53.8 jit_solution(3169332676080174077)
XLA Ops:
  0.6 51.2 %shard_map.68 = (bf16[288,256]{1,0:T(8,128)(2,1)}, bf16[256,1280]{1,0:T(8,128)(2,1)}) custom-call(bf16[288,256]{1,0:T(8,128)(2,1)} %dosage_hbm.1, f32[1,256]{1,0:T(1,128)} %bitcast.3, f32[64,288]{1,0:T(8,128)} %bitcast.2, bf16[288,256]{1,0:T(8,128)(2,1)} %prev_hbm.1, bf16[4608,1280]{1,0:T(8,128)(2,1)} %expr_hbm.1), custom_call_target="tpu_custom_call" | custom-call | tf_op jit(solution)/shard_map/pallas_call | solution.py:337
  51.8 2.0 %shard_map.69 = (bf16[288,256]{1,0:T(8,128)(2,1)}, bf16[256,1280]{1,0:T(8,128)(2,1)}) custom-call(bf16[288,256]{1,0:T(8,128)(2,1)} %get-tuple-element.4.resid_in, bf16[256,1280]{1,0:T(8,128)(2,1)} %get-tuple-element.5.z_in), custom_call_target="tpu_custom_call" | custom-call | tf_op jit(solution)/shard_map/pallas_call | solution.py:376
